TPU v7x, 32 devices: a whole 2x2x4 slice. The times are simulated.
32 devices in a mesh: sc: 4 (over y, x), rows: 8 (over z, core).
Axes of the slice: x: 2, y: 2, z: 4, core: 2. Of those that a mesh axis runs over, the one named last changes fastest.
Arguments:
- embeddings: bfloat16 [32768, 1024], P(('sc', 'rows')), may hold values from -6 to 6
- labels: int32 [32768, 1], P(('sc', 'rows')), may hold values from 0 to 3; in each aligned block of 1024 rows (0 to 1023, 1024 to 2047, ...) at most 512 rows name the same one
- init_idx: int32 [4, 256], P('sc'), may hold values from 0 to 16383
Outputs:
- assign: bfloat16 [32768, 256], P(('sc', 'rows'))
- centroids: float32 [4, 256, 1024], P('sc')
Inputs may be any that keep to these rules, and one draw needn't show every extreme that they name: `labels`: among the rows of one device (aligned blocks of 1024 rows) no label occurs more than 512 times, and some label occurs exactly 512 times; every label occurs somewhere.
All inputs are finite; a program needn't handle non-finite values.
Results may differ from a plain program's by a relative error of at most 0.0052.
Values may be sent and summed in bfloat16 or wider, within the bound.
A program may use at most 64 MiB of HBM per device.

v0:
```python
import math
import jax
import jax.numpy as jnp
from jax import lax
from jax.sharding import PartitionSpec as P

ITERS = 3
ROUNDS = 3


def carried_in(part, axis, combine, identity):
    place = lax.axis_index(axis)
    gathered = lax.all_gather(part, axis)
    state = jnp.zeros_like(part) + jnp.asarray(identity, part.dtype)

    def one(turn, state):
        return combine(state, lax.dynamic_index_in_dim(gathered, turn, 0, False))

    return lax.fori_loop(0, place, one, state)


def unit_of(rows):
    values = rows.astype(jnp.float32)
    scale = lax.rsqrt(jnp.mean(values * values, axis=1, keepdims=True) + 1e-05) * (
        1.0 / math.sqrt(rows.shape[1])
    )
    return (values * scale).astype(jnp.bfloat16)


def unit_cent(mass):
    return (mass * lax.rsqrt(jnp.sum(mass * mass, axis=1, keepdims=True) + 1e-06)).astype(
        jnp.bfloat16
    )


def on_device(embeddings, labels, init_idx):
    tok = embeddings.shape[0]
    width = embeddings.shape[1]
    groups = lax.axis_size("sc")
    slots = 2 * tok // groups
    label_col = labels[:, 0]
    member = (label_col[:, None] == jnp.arange(groups, dtype=jnp.int32)[None, :]).astype(jnp.int32)
    before_here = jnp.cumsum(member, axis=0) - member
    place = jnp.sum(before_here * member, axis=1)
    counts = jnp.sum(member, axis=0).astype(jnp.float32)
    prefix = carried_in(
        counts, ("sc", "rows"), lambda early, later: early + later, jnp.zeros_like(counts)
    )
    totals = lax.psum(counts, ("sc", "rows"))
    prefix_int = prefix.astype(jnp.int32)
    totals_int = totals.astype(jnp.int32)
    rank = jnp.sum(member * prefix_int[None, :], axis=1) + place
    target = label_col * slots + place
    source = (
        jnp.full((groups * slots,), tok, jnp.int32).at[target].set(jnp.arange(tok, dtype=jnp.int32))
    )
    padded = jnp.concatenate([embeddings, jnp.zeros((1, width), jnp.bfloat16)], axis=0)
    rank_pad = jnp.concatenate([rank, jnp.full((1,), -1, jnp.int32)], axis=0)
    outgoing = padded[source].reshape(groups, slots, width)
    out_rank = rank_pad[source].reshape(groups, slots)
    incoming, in_rank = (
        lax.all_to_all(outgoing, "sc", split_axis=0, concat_axis=0, tiled=True),
        lax.all_to_all(out_rank, "sc", split_axis=0, concat_axis=0, tiled=True),
    )
    incoming = incoming.reshape(groups * slots, width)
    in_rank = in_rank.reshape(groups * slots)
    valid = in_rank >= 0
    members = unit_of(incoming)
    group_here = lax.axis_index("sc")
    count = jnp.sum(jnp.where(jnp.arange(groups, dtype=jnp.int32) == group_here, totals_int, 0))
    wanted = init_idx[0] % count
    picker = (wanted[:, None] == in_rank[None, :]).astype(jnp.bfloat16)
    seeds = jnp.dot(picker, members, preferred_element_type=jnp.float32)
    cent = lax.psum(seeds, "rows").astype(jnp.bfloat16)
    contract_rows = (((0,), (0,)), ((), ()))
    contract_width = (((1,), (1,)), ((), ()))
    for round_index in range(ROUNDS):
        scores = lax.dot_general(members, cent, contract_width, preferred_element_type=jnp.float32)
        plan = jnp.where(valid[:, None], jnp.exp(scores * 10.0), 0.0)
        for step in range(ITERS):
            column = lax.psum(jnp.sum(plan, axis=0), "rows")
            plan = plan / column[None, :]
            row_sum = jnp.sum(plan, axis=1)
            plan = jnp.where(valid[:, None], plan / jnp.where(valid, row_sum, 1.0)[:, None], 0.0)
        plan_b = plan.astype(jnp.bfloat16)
        mass_part = lax.dot_general(
            plan_b, members, contract_rows, preferred_element_type=jnp.float32
        )
        if round_index < ROUNDS - 1:
            mass = lax.psum(mass_part, "rows")
            cent = unit_cent(mass)
        else:
            weight_part = jnp.sum(plan, axis=0)
            mass, weight = lax.psum((mass_part, weight_part), "rows")
            means = mass / weight[:, None]
    plan_out = plan.astype(jnp.bfloat16).reshape(groups, slots, plan.shape[1])
    returned = lax.all_to_all(plan_out, "sc", split_axis=0, concat_axis=0, tiled=True).reshape(
        groups * slots, plan.shape[1]
    )
    assign = returned[target]
    return (assign, means[None])


def solution(mesh):
    return jax.shard_map(
        on_device,
        mesh=mesh,
        in_specs=(P(("sc", "rows"), None), P(("sc", "rows"), None), P("sc", None)),
        out_specs=(P(("sc", "rows"), None), P("sc", None, None)),
        check_vma=False,
    )
```

profile of v0, /device:TPU:0, one launch (start us, length us, event | category | flops | bytes accessed | tf_op | source)
XLA Modules:
  0.0 568.7 jit_solution(1118507430221130394)
XLA Ops:
  7.2 0.8 convert_reduce_fusion
  8.1 42.0 %all-reduce.2 = (f32[128]{0:T(128)S(1)}, f32[4]{0:T(128)S(1)}) all-reduce(f32[128]{0:T(128)S(1)} %convert_dynamic-update-slice_fusion, f32[4]{0:T(128)S(1)} %convert_element_type.59), channel_id=2, replica_groups=mesh['sc'=4,'rows'=8] {'sc','rows'}, use_global_device_ids=true, to_apply=%add.1 | all-reduce | flops 132 | bytes 1056
  50.2 0.7 fusion.26
  50.9 1.1 reduce-window.6
  52.0 0.2 slice_reduce_fusion
  52.3 0.2 reduce-window.9
  52.5 0.8 select_reduce_fusion
  53.3 0.7 compare_select_fusion
  54.0 4.3 scatter_custom_fusion
  58.4 20.6 %gather_fusion = s32[2048]{0:T(1024)} fusion(s32[1025]{0:T(1024)S(1)} %pad_add_fusion, s32[2048]{0:T(1024)S(1)} %fusion.27), kind=kCustom, calls=%fused_computation | custom fusion | bytes 24576 | tf_op jit(solution)/shard_map/gather | solution.py:60
  78.9 4.4 all-to-all-start
  83.3 1.8 concatenate.7
  85.1 9.7 %gather_fusion.1 = bf16[2048,1024]{1,0:T(8,128)(2,1)} fusion(bf16[1025,1024]{1,0:T(8,128)(2,1)S(1)} %concatenate.7, s32[2048]{0:T(1024)S(1)} %fusion.27), kind=kCustom, calls=%fused_computation.1 | custom fusion | bytes 8396800 | tf_op jit(solution)/shard_map/gather | solution.py:59
  94.8 5.0 all-to-all-start.1
  99.8 0.6 fusion.30
  101.8 0.1 broadcast_remainder_fusion
  101.9 44.5 %all-to-all-done.1 = bf16[4,512,1024]{2,1,0:T(8,128)(2,1)} async-done(((bf16[4,512,1024]{2,1,0:T(8,128)(2,1)}), bf16[4,512,1024]{2,1,0:T(8,128)(2,1)}, u32[]{:S(2)}, u32[]{:S(2)}) %all-to-all-start.1) | async-done | bytes 4194336 | tf_op jit(solution)/shard_map/all_to_all | solution.py:62
  146.5 3.1 multiply_reduce_fusion
  149.6 2.9 fusion
  152.5 1.9 copy-done.6
  154.4 1.3 fusion.7
  155.8 57.9 %all-reduce.13 = bf16[256,1024]{1,0:T(8,128)(2,1)S(1)} all-reduce(f32[256,1024]{1,0:T(8,128)S(1)} %fusion.7), channel_id=1, replica_groups=mesh['sc'=4,'rows'=8] {'rows'}, use_global_device_ids=true, to_apply=%region_11.12 | all-reduce | flops 262144 | bytes 1572864 | tf_op jit(solution)/shard_map/psum | solution.py:74
  213.7 3.2 fusion.41
  216.8 15.1 %psum.107 = f32[256]{0:T(256)S(1)} all-reduce(f32[256]{0:T(256)S(1)} %get-tuple-element.52), channel_id=1, replica_groups=mesh['sc'=4,'rows'=8] {'rows'}, use_global_device_ids=true, to_apply=%region_13.14 | all-reduce | flops 256 | bytes 2048 | tf_op jit(solution)/shard_map/psum | solution.py:81
  232.0 0.3 divide_reduce_fusion.8
  232.3 2.0 fusion.40
  234.3 13.6 %psum.108 = f32[256]{0:T(256)S(1)} all-reduce(f32[256]{0:T(256)S(1)} %get-tuple-element.48), channel_id=1, replica_groups=mesh['sc'=4,'rows'=8] {'rows'}, use_global_device_ids=true, to_apply=%region_16.17 | all-reduce | flops 256 | bytes 2048 | tf_op jit(solution)/shard_map/psum | solution.py:81
  247.9 0.3 divide_reduce_fusion.7
  248.3 1.7 fusion.39
  250.0 13.7 %psum.109 = f32[256]{0:T(256)S(1)} all-reduce(f32[256]{0:T(256)S(1)} %get-tuple-element.46), channel_id=1, replica_groups=mesh['sc'=4,'rows'=8] {'rows'}, use_global_device_ids=true, to_apply=%region_19.20 | all-reduce | flops 256 | bytes 2048 | tf_op jit(solution)/shard_map/psum | solution.py:81
  263.7 1.9 divide_reduce_fusion.6
  265.7 4.9 fusion.9
  270.6 0.2 all-reduce.10.cloned.1.call-start
  270.9 56.0 %all-reduce.8.cloned.1.call-done = f32[256,1024]{1,0:T(8,128)} async-done(((f32[256,1024]{1,0:T(8,128)}), f32[256,1024]{1,0:T(8,128)}) %all-reduce.8.cloned.1.call-update) | async-done | bytes 1048592 | tf_op jit(solution)/shard_map/psum | solution.py:90
  326.8 1.4 multiply_reduce_fusion.2
  328.2 3.6 fusion.42
  331.8 13.6 %psum.111 = f32[256]{0:T(256)S(1)} all-reduce(f32[256]{0:T(256)S(1)} %get-tuple-element.54), channel_id=1, replica_groups=mesh['sc'=4,'rows'=8] {'rows'}, use_global_device_ids=true, to_apply=%region_24.25 | all-reduce | flops 256 | bytes 2048 | tf_op jit(solution)/shard_map/psum | solution.py:81
  345.4 0.3 divide_reduce_fusion.5
  345.8 2.0 fusion.38
  347.7 13.6 %psum.112 = f32[256]{0:T(256)S(1)} all-reduce(f32[256]{0:T(256)S(1)} %get-tuple-element.44), channel_id=1, replica_groups=mesh['sc'=4,'rows'=8] {'rows'}, use_global_device_ids=true, to_apply=%region_27.28 | all-reduce | flops 256 | bytes 2048 | tf_op jit(solution)/shard_map/psum | solution.py:81
  361.3 0.3 divide_reduce_fusion.4
  361.7 1.7 fusion.37
  363.4 13.7 %psum.113 = f32[256]{0:T(256)S(1)} all-reduce(f32[256]{0:T(256)S(1)} %get-tuple-element.42), channel_id=1, replica_groups=mesh['sc'=4,'rows'=8] {'rows'}, use_global_device_ids=true, to_apply=%region_30.31 | all-reduce | flops 256 | bytes 2048 | tf_op jit(solution)/shard_map/psum | solution.py:81
  377.1 1.9 divide_reduce_fusion.3
  379.1 4.9 fusion.10
  384.1 57.0 %all-reduce.10.cloned.1.call-done = f32[256,1024]{1,0:T(8,128)} async-done(((f32[256,1024]{1,0:T(8,128)}), f32[256,1024]{1,0:T(8,128)}) %all-reduce.10.cloned.1.call-update) | async-done | bytes 1048592 | tf_op jit(solution)/shard_map/psum | solution.py:90
  441.1 1.4 multiply_reduce_fusion.1
  442.5 3.6 fusion.43
  446.1 13.6 %psum.115 = f32[256]{0:T(256)S(1)} all-reduce(f32[256]{0:T(256)S(1)} %get-tuple-element.56), channel_id=1, replica_groups=mesh['sc'=4,'rows'=8] {'rows'}, use_global_device_ids=true, to_apply=%region_35.36 | all-reduce | flops 256 | bytes 2048 | tf_op jit(solution)/shard_map/psum | solution.py:81
  459.7 0.3 divide_reduce_fusion.2
  460.1 2.0 fusion.36
  462.1 13.6 %psum.116 = f32[256]{0:T(256)S(1)} all-reduce(f32[256]{0:T(256)S(1)} %get-tuple-element.40), channel_id=1, replica_groups=mesh['sc'=4,'rows'=8] {'rows'}, use_global_device_ids=true, to_apply=%region_38.39 | all-reduce | flops 256 | bytes 2048 | tf_op jit(solution)/shard_map/psum | solution.py:81
  475.7 0.3 divide_reduce_fusion.1
  476.0 2.0 fusion.35
  478.0 13.6 %psum.117 = f32[256]{0:T(256)S(1)} all-reduce(f32[256]{0:T(256)S(1)} %get-tuple-element.38), channel_id=1, replica_groups=mesh['sc'=4,'rows'=8] {'rows'}, use_global_device_ids=true, to_apply=%region_41.42 | all-reduce | flops 256 | bytes 2048 | tf_op jit(solution)/shard_map/psum | solution.py:81
  491.6 0.3 divide_reduce_fusion
  492.0 1.5 fusion.33
  493.5 0.7 copy-done.7
  494.2 3.5 fusion.44
  497.7 3.6 all-to-all-start.2
  501.3 13.9 %psum.119 = f32[256]{0:T(256)S(1)} all-reduce(f32[256]{0:T(256)S(1)} %get-tuple-element.50), channel_id=1, replica_groups=mesh['sc'=4,'rows'=8] {'rows'}, use_global_device_ids=true, to_apply=%region_45.46 | all-reduce | flops 256 | bytes 2048 | tf_op jit(solution)/shard_map/psum | solution.py:94
  515.2 39.6 %all-reduce.12.cloned.1.call-done = f32[256,1024]{1,0:T(8,128)} async-done(((f32[256,1024]{1,0:T(8,128)}), f32[256,1024]{1,0:T(8,128)}) %all-reduce.12.cloned.1.call-update) | async-done | bytes 1048592 | tf_op jit(solution)/shard_map/psum | solution.py:94
  554.8 2.3 divide_bitcast_fusion
  557.2 5.0 gather_fusion.2
  (51 shorter events, 0.6 us)
Async XLA Ops:
  78.9 15.9 %all-to-all-start = ((s32[4,1,512]{2,1,0:T(1,128)}), s32[4,1,512]{2,1,0:T(1,128)S(1)}, u32[]{:S(2)}, u32[]{:S(2)}) async-start(s32[4,1,512]{2,1,0:T(1,128)} %bitcast.6), calls=%async_computation | async-start | bytes 16384 | tf_op jit(solution)/shard_map/all_to_all | solution.py:63
  94.8 7.0 %copy-start.8 = (s32[1,256]{1,0:T(1,128)S(1)}, s32[1,256]{1,0:T(1,128)}, u32[]{:S(2)}) copy-start(s32[1,256]{1,0:T(1,128)} %param.7) | copy-start | bytes 3076
  94.8 51.7 %all-to-all-start.1 = ((bf16[4,512,1024]{2,1,0:T(8,128)(2,1)}), bf16[4,512,1024]{2,1,0:T(8,128)(2,1)}, u32[]{:S(2)}, u32[]{:S(2)}) async-start(bf16[4,512,1024]{2,1,0:T(8,128)(2,1)} %bitcast.45), calls=%async_computation.1 | async-start | bytes 8388608 | tf_op jit(solution)/shard_map/all_to_all | solution.py:62
  99.8 227.1 %all-reduce.8.cloned.1.call-start = ((), (), s32[]{:S(2)}) async-start(), calls=%async_computation.3 | async-start | bytes 2097152 | tf_op jit(solution)/shard_map/psum | solution.py:90
  152.5 1.9 copy-start.6
  216.8 15.5 %copy-start.3 = (f32[2048,256]{1,0:T(8,128)}, f32[2048,256]{1,0:T(8,128)S(1)}, u32[]{:S(2)}) copy-start(f32[2048,256]{1,0:T(8,128)S(1)} %get-tuple-element.53) | copy-start | bytes 6291460
  250.0 15.7 %copy-start.4 = (f32[2048,256]{1,0:T(8,128)S(1)}, f32[2048,256]{1,0:T(8,128)}, u32[]{:S(2)}) copy-start(f32[2048,256]{1,0:T(8,128)} %get-tuple-element.47) | copy-start | bytes 6291460
  270.6 170.5 %all-reduce.10.cloned.1.call-start = ((), (), s32[]{:S(2)}) async-start(), calls=%async_computation.4 | async-start | bytes 2097152 | tf_op jit(solution)/shard_map/psum | solution.py:90
  331.8 14.0 %copy-start.1 = (f32[2048,256]{1,0:T(8,128)}, f32[2048,256]{1,0:T(8,128)S(1)}, u32[]{:S(2)}) copy-start(f32[2048,256]{1,0:T(8,128)S(1)} %get-tuple-element.55) | copy-start | bytes 6291460
  363.4 15.7 %copy-start.5 = (f32[2048,256]{1,0:T(8,128)S(1)}, f32[2048,256]{1,0:T(8,128)}, u32[]{:S(2)}) copy-start(f32[2048,256]{1,0:T(8,128)} %get-tuple-element.43) | copy-start | bytes 6291460
  384.1 170.8 %all-reduce.12.cloned.1.call-start = ((), (), s32[]{:S(2)}) async-start(), calls=%async_computation.5 | async-start | bytes 2097152 | tf_op jit(solution)/shard_map/psum | solution.py:94
  446.1 14.0 %copy-start.2 = (f32[2048,256]{1,0:T(8,128)}, f32[2048,256]{1,0:T(8,128)S(1)}, u32[]{:S(2)}) copy-start(f32[2048,256]{1,0:T(8,128)S(1)} %get-tuple-element.57) | copy-start | bytes 6291460
  462.1 14.0 %copy-start = (f32[2048,256]{1,0:T(8,128)}, f32[2048,256]{1,0:T(8,128)S(1)}, u32[]{:S(2)}) copy-start(f32[2048,256]{1,0:T(8,128)S(1)} %get-tuple-element.41) | copy-start | bytes 6291460
  491.6 2.6 copy-start.7
  497.7 59.5 %all-to-all-start.2 = ((bf16[4,512,256]{2,1,0:T(8,128)(2,1)}), bf16[4,512,256]{2,1,0:T(8,128)(2,1)S(1)}, u32[]{:S(2)}, u32[]{:S(2)}) async-start(bf16[4,512,256]{2,1,0:T(8,128)(2,1)} %bitcast.11), calls=%async_computation.2 | async-start | bytes 2097152 | tf_op jit(solution)/shard_map/all_to_all | solution.py:97
Sparse Core Ops, SparseCore 0:
  270.8 56.0 all-reduce.7
  384.2 56.9 all-reduce.9
  497.8 56.9 all-reduce.11
where the time goes:
time: 570 us; the launch traced here: 569 us
  blocking collectives  238 us (42%)
  waiting for transfers between devices  197 us (35%)
  local copies, waits for them, and re-layouts  44.2 us (8%)
  other arithmetic  35.6 us (6%)
  matrix products  25 us (4%)
  between operations  15.5 us (3%)
  starting transfers between devices  13.4 us (2%)
    psum x9, blocking collectives, on_device(): column = lax.psum(jnp.sum(plan, axis=0), 'rows')  124 us
    psum x2, waiting for transfers between devices, on_device(): mass = lax.psum(mass_part, 'rows')  113 us
    psum x1, blocking collectives, on_device(): cent = lax.psum(seeds, 'rows').astype(jnp.bfloat16)  57.9 us
    all_to_all x1, waiting for transfers between devices, on_device(): lax.all_to_all(outgoing, 'sc', split_axis=0, concat_axis=0, tiled=True)  44.5 us
    unnamed x1, blocking collectives  42 us
    psum x1, waiting for transfers between devices, on_device(): mass, weight = lax.psum((mass_part, weight_part), 'rows')  39.6 us
    gather x1, local copies, waits for them, and re-layouts, on_device(): out_rank = rank_pad[source].reshape(groups, slots)  20.6 us
    psum x1, blocking collectives, on_device(): mass, weight = lax.psum((mass_part, weight_part), 'rows')  13.9 us
  transfers between devices with their start and end apart: 6, of which 4 were waited for; matrix products, arithmetic and copies ran while one was open for 3% of the time, Pallas kernels for 0%

commit v1 on v0

--- a/solution.py
+++ b/solution.py
@@ -6,6 +6,18 @@
 
 ITERS = 3
 ROUNDS = 3
+
+
+def exchange_directly(x, axis, split, join):
+    ways, here = (lax.axis_size(axis), lax.axis_index(axis))
+    width = x.shape[split] // ways
+    turned = jnp.roll(x, -here * width, axis=split)
+    got = [lax.slice_in_dim(turned, 0, width, axis=split)]
+    for far in range(1, ways):
+        sent = lax.slice_in_dim(turned, far * width, (far + 1) * width, axis=split)
+        got.append(lax.ppermute(sent, axis, [(d, (d + far) % ways) for d in range(ways)]))
+    line = jnp.concatenate(got[::-1], axis=join)
+    return jnp.roll(line, (here + 1) * got[0].shape[join], axis=join)
 
 
 def carried_in(part, axis, combine, identity):
@@ -59,7 +71,7 @@
     outgoing = padded[source].reshape(groups, slots, width)
     out_rank = rank_pad[source].reshape(groups, slots)
     incoming, in_rank = (
-        lax.all_to_all(outgoing, "sc", split_axis=0, concat_axis=0, tiled=True),
+        exchange_directly(outgoing, "sc", 0, 0),
         lax.all_to_all(out_rank, "sc", split_axis=0, concat_axis=0, tiled=True),
     )
     incoming = incoming.reshape(groups * slots, width)

time: 570 us -> 550 us (0.965)
  waiting for transfers between devices: 197 us -> 172 us
    all_to_all x1 -> x0, waiting for transfers between devices: 44.5 us -> none  [on_device(): lax.all_to_all(outgoing, 'sc', split_axis=0, concat_axis=0, tiled=True)]
    all_to_all x1, waiting for transfers between devices: 0.01 us -> 19 us  [on_device(): lax.all_to_all(out_rank, 'sc', split_axis=0, concat_axis=0, tiled=True)]
  transfers between devices with their start and end apart: 6 -> 8, of which waited for: 4 -> 4; matrix products, arithmetic and copies ran while one was open for 3% -> 4% of each run, Pallas kernels for 0% -> 0%
where the time goes in v1:
time: 550 us; the launch traced here: 549 us
  blocking collectives  238 us (43%)
  waiting for transfers between devices  172 us (31%)
  local copies, waits for them, and re-layouts  46 us (8%)
  other arithmetic  40.6 us (7%)
  matrix products  25 us (5%)
  between operations  15.3 us (3%)
  starting transfers between devices  11.9 us (2%)
    psum x9, blocking collectives, on_device(): column = lax.psum(jnp.sum(plan, axis=0), 'rows')  124 us
    psum x2, waiting for transfers between devices, on_device(): mass = lax.psum(mass_part, 'rows')  114 us
    psum x1, blocking collectives, on_device(): cent = lax.psum(seeds, 'rows').astype(jnp.bfloat16)  57.8 us
    unnamed x1, blocking collectives  42 us
    psum x1, waiting for transfers between devices, on_device(): mass, weight = lax.psum((mass_part, weight_part), 'rows')  39.6 us
    gather x1, local copies, waits for them, and re-layouts, on_device(): out_rank = rank_pad[source].reshape(groups, slots)  20.6 us
    all_to_all x1, waiting for transfers between devices, on_device(): lax.all_to_all(out_rank, 'sc', split_axis=0, concat_axis=0, tiled=True)  19 us
    psum x1, blocking collectives, on_device(): mass, weight = lax.psum((mass_part, weight_part), 'rows')  13.9 us
  transfers between devices with their start and end apart: 8, of which 4 were waited for; matrix products, arithmetic and copies ran while one was open for 4% of the time, Pallas kernels for 0%

profile of v1, /device:TPU:0, one launch (start us, length us, event | category | flops | bytes accessed | tf_op | source)
XLA Modules:
  0.0 549.2 jit_solution(15746547357838925265)
XLA Ops:
  7.2 0.8 convert_reduce_fusion
  8.1 42.0 %all-reduce.2 = (f32[128]{0:T(128)S(1)}, f32[4]{0:T(128)S(1)}) all-reduce(f32[128]{0:T(128)S(1)} %convert_dynamic-update-slice_fusion, f32[4]{0:T(128)S(1)} %convert_element_type.59), channel_id=2, replica_groups=mesh['sc'=4,'rows'=8] {'sc','rows'}, use_global_device_ids=true, to_apply=%add.1 | all-reduce | flops 132 | bytes 1056
  50.2 0.7 fusion.35
  50.9 1.1 reduce-window.6
  52.0 0.2 slice_reduce_fusion
  52.5 0.8 select_reduce_fusion
  53.3 0.7 compare_select_fusion
  54.0 4.3 scatter_custom_fusion
  58.4 1.8 concatenate.13
  60.1 9.7 %gather_fusion.1 = bf16[2048,1024]{1,0:T(8,128)(2,1)} fusion(bf16[1025,1024]{1,0:T(8,128)(2,1)S(1)} %concatenate.13, s32[2048]{0:T(1024)S(1)} %fusion.36), kind=kCustom, calls=%fused_computation.1 | custom fusion | bytes 8396800 | tf_op jit(solution)/shard_map/gather | solution.py:71
  69.8 3.1 fusion.9
  72.9 1.8 fusion.51
  74.7 3.1 collective-permute-start
  77.8 1.8 collective-permute-start.1
  79.6 20.6 %gather_fusion = s32[2048]{0:T(1024)} fusion(s32[1025]{0:T(1024)S(1)} %pad_add_fusion, s32[2048]{0:T(1024)S(1)} %fusion.36), kind=kCustom, calls=%fused_computation | custom fusion | bytes 24576 | tf_op jit(solution)/shard_map/gather | solution.py:72
  100.2 3.3 all-to-all-start
  103.5 0.6 fusion.39
  105.4 19.0 %all-to-all-done = s32[4,1,512]{2,1,0:T(1,128)S(1)} async-done(((s32[4,1,512]{2,1,0:T(1,128)}), s32[4,1,512]{2,1,0:T(1,128)S(1)}, u32[]{:S(2)}, u32[]{:S(2)}) %all-to-all-start) | async-done | bytes 8224 | tf_op jit(solution)/shard_map/all_to_all | solution.py:75
  124.4 7.5 %multiply_reduce_fusion = (f32[4,512]{1,0:T(4,128)S(1)}, f32[4,512,1024]{2,1,0:T(8,128)S(1)}) fusion(s32[]{:T(128)S(6)} %select_n.171, bf16[1,512,1024]{2,1,0:T(8,128)(2,1)S(1)} %get-tuple-element.56, bf16[1,512,1024]{2,1,0:T(8,128)(2,1)} %collective-permute-done.2, bf16[1,512,1024]{2,1,0:T(8,128)(2,1)} %collective-permute-done.1, ...), kind=kLoop, calls=%fused_computation.17 | loop fusion | flops 20969472 | bytes 12591108 | tf_op jit(solution)/shard_map/reduce_sum | solution.py:36
  131.9 0.5 fusion
  132.4 1.9 copy-done.6
  134.3 1.3 fusion.16
  135.6 57.8 %all-reduce.13 = bf16[256,1024]{1,0:T(8,128)(2,1)S(1)} all-reduce(f32[256,1024]{1,0:T(8,128)S(1)} %fusion.16), channel_id=1, replica_groups=mesh['sc'=4,'rows'=8] {'rows'}, use_global_device_ids=true, to_apply=%region_11.13 | all-reduce | flops 262144 | bytes 1572864 | tf_op jit(solution)/shard_map/psum | solution.py:86
  193.4 3.1 fusion.52
  196.6 15.3 %psum.107 = f32[256]{0:T(256)S(1)} all-reduce(f32[256]{0:T(256)S(1)} %get-tuple-element.59), channel_id=1, replica_groups=mesh['sc'=4,'rows'=8] {'rows'}, use_global_device_ids=true, to_apply=%region_13.15 | all-reduce | flops 256 | bytes 2048 | tf_op jit(solution)/shard_map/psum | solution.py:93
  211.9 0.3 divide_reduce_fusion.8
  212.2 2.0 fusion.49
  214.2 13.6 %psum.108 = f32[256]{0:T(256)S(1)} all-reduce(f32[256]{0:T(256)S(1)} %get-tuple-element.49), channel_id=1, replica_groups=mesh['sc'=4,'rows'=8] {'rows'}, use_global_device_ids=true, to_apply=%region_16.18 | all-reduce | flops 256 | bytes 2048 | tf_op jit(solution)/shard_map/psum | solution.py:93
  227.8 0.3 divide_reduce_fusion.7
  228.2 1.7 fusion.48
  229.9 13.9 %psum.109 = f32[256]{0:T(256)S(1)} all-reduce(f32[256]{0:T(256)S(1)} %get-tuple-element.47), channel_id=1, replica_groups=mesh['sc'=4,'rows'=8] {'rows'}, use_global_device_ids=true, to_apply=%region_19.21 | all-reduce | flops 256 | bytes 2048 | tf_op jit(solution)/shard_map/psum | solution.py:93
  243.8 1.9 divide_reduce_fusion.6
  245.7 4.9 fusion.18
  250.7 56.6 %all-reduce.8.cloned.1.call-done = f32[256,1024]{1,0:T(8,128)} async-done(((f32[256,1024]{1,0:T(8,128)}), f32[256,1024]{1,0:T(8,128)}) %all-reduce.8.cloned.1.call-update) | async-done | bytes 1048592 | tf_op jit(solution)/shard_map/psum | solution.py:102
  307.3 1.4 multiply_reduce_fusion.2
  308.7 3.6 fusion.53
  312.3 13.6 %psum.111 = f32[256]{0:T(256)S(1)} all-reduce(f32[256]{0:T(256)S(1)} %get-tuple-element.61), channel_id=1, replica_groups=mesh['sc'=4,'rows'=8] {'rows'}, use_global_device_ids=true, to_apply=%region_24.26 | all-reduce | flops 256 | bytes 2048 | tf_op jit(solution)/shard_map/psum | solution.py:93
  325.9 0.3 divide_reduce_fusion.5
  326.3 2.0 fusion.47
  328.2 13.6 %psum.112 = f32[256]{0:T(256)S(1)} all-reduce(f32[256]{0:T(256)S(1)} %get-tuple-element.45), channel_id=1, replica_groups=mesh['sc'=4,'rows'=8] {'rows'}, use_global_device_ids=true, to_apply=%region_27.29 | all-reduce | flops 256 | bytes 2048 | tf_op jit(solution)/shard_map/psum | solution.py:93
  341.8 0.3 divide_reduce_fusion.4
  342.2 1.7 fusion.46
  343.9 13.7 %psum.113 = f32[256]{0:T(256)S(1)} all-reduce(f32[256]{0:T(256)S(1)} %get-tuple-element.43), channel_id=1, replica_groups=mesh['sc'=4,'rows'=8] {'rows'}, use_global_device_ids=true, to_apply=%region_30.32 | all-reduce | flops 256 | bytes 2048 | tf_op jit(solution)/shard_map/psum | solution.py:93
  357.6 1.9 divide_reduce_fusion.3
  359.6 4.9 fusion.19
  364.6 57.1 %all-reduce.10.cloned.1.call-done = f32[256,1024]{1,0:T(8,128)} async-done(((f32[256,1024]{1,0:T(8,128)}), f32[256,1024]{1,0:T(8,128)}) %all-reduce.10.cloned.1.call-update) | async-done | bytes 1048592 | tf_op jit(solution)/shard_map/psum | solution.py:102
  421.7 1.4 multiply_reduce_fusion.1
  423.1 3.6 fusion.54
  426.7 13.6 %psum.115 = f32[256]{0:T(256)S(1)} all-reduce(f32[256]{0:T(256)S(1)} %get-tuple-element.63), channel_id=1, replica_groups=mesh['sc'=4,'rows'=8] {'rows'}, use_global_device_ids=true, to_apply=%region_35.37 | all-reduce | flops 256 | bytes 2048 | tf_op jit(solution)/shard_map/psum | solution.py:93
  440.3 0.3 divide_reduce_fusion.2
  440.6 2.0 fusion.45
  442.6 13.6 %psum.116 = f32[256]{0:T(256)S(1)} all-reduce(f32[256]{0:T(256)S(1)} %get-tuple-element.41), channel_id=1, replica_groups=mesh['sc'=4,'rows'=8] {'rows'}, use_global_device_ids=true, to_apply=%region_38.40 | all-reduce | flops 256 | bytes 2048 | tf_op jit(solution)/shard_map/psum | solution.py:93
  456.2 0.3 divide_reduce_fusion.1
  456.6 2.0 fusion.44
  458.6 13.6 %psum.117 = f32[256]{0:T(256)S(1)} all-reduce(f32[256]{0:T(256)S(1)} %get-tuple-element.39), channel_id=1, replica_groups=mesh['sc'=4,'rows'=8] {'rows'}, use_global_device_ids=true, to_apply=%region_41.43 | all-reduce | flops 256 | bytes 2048 | tf_op jit(solution)/shard_map/psum | solution.py:93
  472.2 0.3 divide_reduce_fusion
  472.5 1.5 fusion.42
  474.1 0.7 copy-done.7
  474.7 3.5 fusion.55
  478.2 3.6 all-to-all-start.1
  481.9 13.9 %psum.119 = f32[256]{0:T(256)S(1)} all-reduce(f32[256]{0:T(256)S(1)} %get-tuple-element.57), channel_id=1, replica_groups=mesh['sc'=4,'rows'=8] {'rows'}, use_global_device_ids=true, to_apply=%region_45.47 | all-reduce | flops 256 | bytes 2048 | tf_op jit(solution)/shard_map/psum | solution.py:106
  495.8 39.6 %all-reduce.12.cloned.1.call-done = f32[256,1024]{1,0:T(8,128)} async-done(((f32[256,1024]{1,0:T(8,128)}), f32[256,1024]{1,0:T(8,128)}) %all-reduce.12.cloned.1.call-update) | async-done | bytes 1048592 | tf_op jit(solution)/shard_map/psum | solution.py:106
  535.3 2.3 divide_bitcast_fusion
  537.7 5.0 gather_fusion.2
  (57 shorter events, 0.9 us)
Async XLA Ops:
  74.7 49.6 %collective-permute-start = (bf16[1,512,1024]{2,1,0:T(8,128)(2,1)}, bf16[1,512,1024]{2,1,0:T(8,128)(2,1)S(1)}, u32[]{:S(2)}, u32[]{:S(2)}) collective-permute-start(bf16[1,512,1024]{2,1,0:T(8,128)(2,1)} %get-tuple-element.53), channel_id=1, source_target_pairs={{0,24},{8,0},{16,8},{24,16},{1,25},{9,1},{17,9},{25,17},{2,26},{10... | collective-permute-start | bytes 3145736 | tf_op jit(solution)/shard_map/ppermute | solution.py:18
  77.8 46.5 %collective-permute-start.2 = (bf16[1,512,1024]{2,1,0:T(8,128)(2,1)}, bf16[1,512,1024]{2,1,0:T(8,128)(2,1)}, u32[]{:S(2)}, u32[]{:S(2)}) collective-permute-start(bf16[1,512,1024]{2,1,0:T(8,128)(2,1)} %get-tuple-element.54), channel_id=1, source_target_pairs={{0,8},{8,16},{16,24},{24,0},{1,9},{9,17},{17,25},{25,1},{2,10},{10... | collective-permute-start | bytes 3145736 | tf_op jit(solution)/shard_map/ppermute | solution.py:18
  77.8 46.5 %collective-permute-start.1 = (bf16[1,512,1024]{2,1,0:T(8,128)(2,1)S(1)}, bf16[1,512,1024]{2,1,0:T(8,128)(2,1)}, u32[]{:S(2)}, u32[]{:S(2)}) collective-permute-start(bf16[1,512,1024]{2,1,0:T(8,128)(2,1)S(1)} %get-tuple-element.55), channel_id=1, source_target_pairs={{0,16},{8,24},{16,0},{24,8},{1,17},{9,25},{17,1},{25,9},{2,18},{10... | collective-permute-start | bytes 3145736 | tf_op jit(solution)/shard_map/ppermute | solution.py:18
  79.6 25.6 %copy-start.8 = (s32[1,256]{1,0:T(1,128)S(1)}, s32[1,256]{1,0:T(1,128)}, u32[]{:S(2)}) copy-start(s32[1,256]{1,0:T(1,128)} %param.9) | copy-start | bytes 3076
  100.2 24.2 %all-to-all-start = ((s32[4,1,512]{2,1,0:T(1,128)}), s32[4,1,512]{2,1,0:T(1,128)S(1)}, u32[]{:S(2)}, u32[]{:S(2)}) async-start(s32[4,1,512]{2,1,0:T(1,128)} %bitcast.6), calls=%async_computation | async-start | bytes 16384 | tf_op jit(solution)/shard_map/all_to_all | solution.py:75
  103.5 203.8 %all-reduce.8.cloned.1.call-start = ((), (), s32[]{:S(2)}) async-start(), calls=%async_computation.2 | async-start | bytes 2097152 | tf_op jit(solution)/shard_map/psum | solution.py:102
  132.4 1.9 copy-start.6
  196.6 15.6 %copy-start.3 = (f32[2048,256]{1,0:T(8,128)}, f32[2048,256]{1,0:T(8,128)S(1)}, u32[]{:S(2)}) copy-start(f32[2048,256]{1,0:T(8,128)S(1)} %get-tuple-element.60) | copy-start | bytes 6291460
  229.9 15.8 %copy-start.4 = (f32[2048,256]{1,0:T(8,128)S(1)}, f32[2048,256]{1,0:T(8,128)}, u32[]{:S(2)}) copy-start(f32[2048,256]{1,0:T(8,128)} %get-tuple-element.48) | copy-start | bytes 6291460
  250.7 171.0 %all-reduce.10.cloned.1.call-start = ((), (), s32[]{:S(2)}) async-start(), calls=%async_computation.3 | async-start | bytes 2097152 | tf_op jit(solution)/shard_map/psum | solution.py:102
  312.3 14.0 %copy-start.1 = (f32[2048,256]{1,0:T(8,128)}, f32[2048,256]{1,0:T(8,128)S(1)}, u32[]{:S(2)}) copy-start(f32[2048,256]{1,0:T(8,128)S(1)} %get-tuple-element.62) | copy-start | bytes 6291460
  343.9 15.7 %copy-start.5 = (f32[2048,256]{1,0:T(8,128)S(1)}, f32[2048,256]{1,0:T(8,128)}, u32[]{:S(2)}) copy-start(f32[2048,256]{1,0:T(8,128)} %get-tuple-element.44) | copy-start | bytes 6291460
  364.5 170.8 %all-reduce.12.cloned.1.call-start = ((), (), s32[]{:S(2)}) async-start(), calls=%async_computation.4 | async-start | bytes 2097152 | tf_op jit(solution)/shard_map/psum | solution.py:106
  426.7 14.0 %copy-start.2 = (f32[2048,256]{1,0:T(8,128)}, f32[2048,256]{1,0:T(8,128)S(1)}, u32[]{:S(2)}) copy-start(f32[2048,256]{1,0:T(8,128)S(1)} %get-tuple-element.64) | copy-start | bytes 6291460
  442.6 14.0 %copy-start = (f32[2048,256]{1,0:T(8,128)}, f32[2048,256]{1,0:T(8,128)S(1)}, u32[]{:S(2)}) copy-start(f32[2048,256]{1,0:T(8,128)S(1)} %get-tuple-element.42) | copy-start | bytes 6291460
  472.2 2.6 copy-start.7
  478.2 59.5 %all-to-all-start.1 = ((bf16[4,512,256]{2,1,0:T(8,128)(2,1)}), bf16[4,512,256]{2,1,0:T(8,128)(2,1)S(1)}, u32[]{:S(2)}, u32[]{:S(2)}) async-start(bf16[4,512,256]{2,1,0:T(8,128)(2,1)} %bitcast.11), calls=%async_computation.1 | async-start | bytes 2097152 | tf_op jit(solution)/shard_map/all_to_all | solution.py:109
Sparse Core Ops, SparseCore 0:
  250.8 56.4 all-reduce.7
  364.7 56.9 all-reduce.9
  478.4 56.9 all-reduce.11
